TPU v7x, 128 devices: a whole 4x4x4 slice. The times are simulated.
128 devices in a mesh: tok: 8 (over y, core), head: 16 (over x, z).
Axes of the slice: x: 4, y: 4, z: 4, core: 2. Of those that a mesh axis runs over, the one named last changes fastest.
Arguments:
- hidden_states: bfloat16 [5120, 6144], P('tok', 'head'), may hold values from -6 to 6
- norm_gain: float32 [6144], replicated, may hold values from 0.5 to 1.5
- norm_bias: float32 [6144], replicated, may hold values from -2 to 2
- qkv_weight: bfloat16 [6144, 18432], P('tok', 'head'), may hold values from -0.125 to 0.125
- qkv_bias: bfloat16 [18432], P('head'), may hold values from -2 to 2
- dense_weight: bfloat16 [6144, 6144], P('head'), may hold values from -0.21875 to 0.21875
- dense_bias: bfloat16 [6144], P('head'), may hold values from -2 to 2
- prefix_keys: bfloat16 [16, 2048, 6144], P('tok', None, 'head'), may hold values from -70 to 70
- prefix_values: bfloat16 [16, 2048, 6144], P('tok', None, 'head'), may hold values from -10 to 10
- suffix_len: int32 [8, 16], P('tok'), may hold values from 1 to 120, as said below
- request_order: int32 [8, 16], P('tok'), may hold values from 0 to 15, each once within a row
- group_slot: int32 [16], replicated, may hold values from 0 to 15, each once
Outputs:
- layer_out: bfloat16 [5120, 6144], P('tok', 'head')
Inputs may be any that keep to these rules, and one draw needn't show every extreme that they name: `suffix_len`: each row sums to 640; one group, the same in every row, has exactly 120 in every row. `request_order`: each row names every group once. `group_slot`: each slot holds one group.
All inputs are finite; a program needn't handle non-finite values.
Results may differ from a plain program's by a relative error of at most 0.007.
The roundings to bfloat16 on the way count: a program that leaves them out, or rounds other values in their place, can miss the bound.
Values may be sent and summed in bfloat16 or wider, within the bound.
A program may use at most 128 MiB of HBM per device.

v0:
```python
import jax
import jax.numpy as jnp
from jax import lax
from jax.sharding import PartitionSpec as P

HS = 96


def layer_norm(values_in, gain, shift):
    widened = values_in.astype(jnp.float32)
    center = jnp.mean(widened, axis=-1, keepdims=True)
    spread = jnp.mean(jnp.square(widened - center), axis=-1, keepdims=True)
    return ((widened - center) * lax.rsqrt(spread + 1e-05) * gain + shift).astype(jnp.bfloat16)


def shard_layout(lengths, ordering, row_count):
    group_count = lengths.shape[0]
    labels = jnp.arange(group_count, dtype=jnp.int32)
    chosen = (ordering[:, None] == labels[None, :]).astype(jnp.int32)
    ranking = jnp.sum(labels[:, None] * chosen, axis=0)
    earlier = (ranking[None, :] < ranking[:, None]).astype(jnp.int32)
    starts = jnp.sum(earlier * lengths[None, :], axis=1)
    places = jnp.arange(row_count, dtype=jnp.int32)
    member = (
        (places[:, None] >= starts[None, :]) & (places[:, None] < (starts + lengths)[None, :])
    ).astype(jnp.int32)
    group_of = jnp.sum(member * labels[None, :], axis=1)
    within = places - jnp.sum(member * starts[None, :], axis=1)
    return (starts, member, group_of, within)


def rotary(tensor, positions, rot_dims):
    half_dims = rot_dims // 2
    inverse = 10000.0 ** (-(jnp.arange(half_dims, dtype=jnp.float32) * 2.0) / rot_dims)
    angles = positions.astype(jnp.float32)[:, None] * inverse[None, :]
    cosine = jnp.cos(angles)[:, None, :]
    sine_part = jnp.sin(angles)[:, None, :]
    lower_half = tensor[..., :half_dims]
    upper_half = tensor[..., half_dims:rot_dims]
    return jnp.concatenate(
        [
            lower_half * cosine - upper_half * sine_part,
            upper_half * cosine + lower_half * sine_part,
            tensor[..., rot_dims:],
        ],
        axis=-1,
    )


def local_suffix(queries, keys_new, values_new, group_of):
    scaling = HS ** (-0.5)
    scores = (
        jnp.einsum("ihd,jhd->hij", queries, keys_new, preferred_element_type=jnp.float32) * scaling
    )
    places = jnp.arange(queries.shape[0], dtype=jnp.int32)
    allowed = (group_of[:, None] == group_of[None, :]) & (places[None, :] <= places[:, None])
    masked = jnp.where(allowed[None], scores, -jnp.inf)
    row_peak = jnp.max(masked, axis=-1)
    weights = jnp.exp(masked - row_peak[..., None])
    row_mass = jnp.sum(weights, axis=-1)
    blended = (
        jnp.einsum(
            "hij,jhd->ihd",
            weights.astype(jnp.bfloat16),
            values_new,
            preferred_element_type=jnp.float32,
        )
        / jnp.transpose(row_mass)[..., None]
    )
    return (jnp.transpose(row_peak), jnp.transpose(row_mass), blended)


def prefix_slot(operands):
    queries_in, keys_in, values_in = operands
    row_total = queries_in.shape[0]
    local_width = queries_in.shape[1]
    local_heads = local_width // HS
    prefix_length = keys_in.shape[0]
    query_heads = queries_in.reshape(row_total, local_heads, HS)
    key_heads = keys_in.reshape(prefix_length, local_heads, HS)
    value_heads = values_in.reshape(prefix_length, local_heads, HS)
    scores = jnp.einsum(
        "rhd,phd->hrp", query_heads, key_heads, preferred_element_type=jnp.float32
    ) * HS ** (-0.5)
    row_peak = jnp.max(scores, axis=-1)
    weights = jnp.exp(scores - row_peak[..., None])
    row_mass = jnp.sum(weights, axis=-1)
    blended = (
        jnp.einsum(
            "hrp,phd->rhd",
            weights.astype(jnp.bfloat16),
            value_heads,
            preferred_element_type=jnp.float32,
        )
        / jnp.transpose(row_mass)[..., None]
    )
    return (
        blended.reshape(row_total, local_width),
        jnp.transpose(row_peak),
        jnp.transpose(row_mass),
    )


def on_device(
    hidden_states,
    norm_gain,
    norm_bias,
    qkv_weight,
    qkv_bias,
    dense_weight,
    dense_bias,
    prefix_keys,
    prefix_values,
    suffix_len,
    request_order,
    group_slot,
):
    tok_rows = hidden_states.shape[0]
    slot_local = prefix_keys.shape[0]
    prefix_length = prefix_keys.shape[1]
    local_width = prefix_keys.shape[2]
    local_heads = local_width // HS
    group_count = slot_local * lax.axis_size("tok")
    capacity = 3 * tok_rows // group_count
    full_rows = lax.all_gather(hidden_states, "head", axis=1, tiled=True)
    normed = layer_norm(full_rows, norm_gain, norm_bias)
    projected = jnp.dot(
        normed,
        lax.all_gather(qkv_weight, "tok", axis=0, tiled=True),
        preferred_element_type=jnp.float32,
    )
    projected = (projected + qkv_bias.astype(jnp.float32)).reshape(tok_rows, local_heads, 3, HS)
    lengths = suffix_len[0]
    starts, member, group_of, within = shard_layout(lengths, request_order[0], tok_rows)
    positions = prefix_length + within
    queries = rotary(projected[:, :, 0], positions, HS // 4).astype(jnp.bfloat16)
    keys_new = rotary(projected[:, :, 1], positions, HS // 4).astype(jnp.bfloat16)
    values_new = projected[:, :, 2].astype(jnp.bfloat16)
    suf_peak, suf_mass, suf_out = local_suffix(queries, keys_new, values_new, group_of)
    labels = jnp.arange(group_count, dtype=jnp.int32)
    slot_match = (group_slot[:, None] == labels[None, :]).astype(jnp.int32)
    slot_starts = jnp.sum(starts[:, None] * slot_match, axis=0)
    slot_lengths = jnp.sum(lengths[:, None] * slot_match, axis=0)
    cap_index = jnp.arange(capacity, dtype=jnp.int32)
    live_slot = cap_index[None, :] < slot_lengths[:, None]
    source_rows = jnp.where(live_slot, slot_starts[:, None] + cap_index[None, :], 0)
    flat_query = queries.reshape(tok_rows, local_width)
    outgoing = jnp.where(live_slot[..., None], flat_query[source_rows], jnp.zeros((), jnp.bfloat16))
    incoming = lax.all_to_all(outgoing, "tok", split_axis=0, concat_axis=1, tiled=True)
    pre_all, peak_all, mass_all = lax.map(prefix_slot, (incoming, prefix_keys, prefix_values))
    returned = (
        lax.all_to_all(pre_all, "tok", split_axis=1, concat_axis=0, tiled=True),
        lax.all_to_all(peak_all, "tok", split_axis=1, concat_axis=0, tiled=True),
        lax.all_to_all(mass_all, "tok", split_axis=1, concat_axis=0, tiled=True),
    )
    token_slot = jnp.sum(member * group_slot[None, :], axis=1)
    flat_index = token_slot * capacity + within
    pre_out = returned[0].reshape(group_count * capacity, local_heads, HS)[flat_index]
    pre_peak = returned[1].reshape(group_count * capacity, local_heads)[flat_index]
    pre_mass = returned[2].reshape(group_count * capacity, local_heads)[flat_index]
    joint_peak = jnp.maximum(pre_peak, suf_peak)
    pre_share = pre_mass * jnp.exp(pre_peak - joint_peak)
    suf_share = suf_mass * jnp.exp(suf_peak - joint_peak)
    combined = (pre_share[..., None] * pre_out + suf_share[..., None] * suf_out) / (
        pre_share + suf_share
    )[..., None]
    attention = combined.reshape(tok_rows, local_width).astype(jnp.bfloat16)
    partial_out = jnp.dot(attention, dense_weight, preferred_element_type=jnp.float32)
    summed = lax.psum_scatter(partial_out, "head", scatter_dimension=1, tiled=True)
    return (hidden_states.astype(jnp.float32) + dense_bias.astype(jnp.float32) + summed).astype(
        jnp.bfloat16
    )


def solution(mesh):
    placed = (
        P("tok", "head"),
        P(),
        P(),
        P("tok", "head"),
        P("head"),
        P("head", None),
        P("head"),
        P("tok", None, "head"),
        P("tok", None, "head"),
        P("tok", None),
        P("tok", None),
        P(),
    )
    return jax.shard_map(
        on_device, mesh=mesh, in_specs=placed, out_specs=P("tok", "head"), check_vma=False
    )
```

profile of v0, /device:TPU:1, one launch (start us, length us, event | category | flops | bytes accessed | tf_op | source)
XLA Modules:
  0.0 575.9 jit_solution(17584146502956771030)
XLA Ops:
  8.7 0.8 select_reduce_fusion.4
  9.6 0.8 select_reduce_fusion.6
  11.9 1.3 select_reduce_fusion
  14.1 73.5 %all-gather.3.cloned.1.call-done = bf16[640,6144]{1,0:T(8,128)(2,1)} async-done(((bf16[640,384]{1,0:T(8,128)(2,1)}), bf16[640,6144]{1,0:T(8,128)(2,1)}) %all-gather.3.cloned.1.call-update) | async-done | bytes 7864336 | tf_op jit(solution)/shard_map/all_gather | solution.py:125
  87.7 4.5 convert_reduce_fusion
  92.2 1.0 copy-done.1
  93.1 2.2 fusion.9
  95.3 68.6 %all-gather.5.cloned.1.call-done = bf16[6144,1152]{1,0:T(8,128)(2,1)} async-done(((bf16[768,1152]{1,0:T(8,128)(2,1)}), bf16[6144,1152]{1,0:T(8,128)(2,1)}) %all-gather.5.cloned.1.call-update) | async-done | bytes 14155792 | tf_op jit(solution)/shard_map/all_gather | solution.py:129
  163.9 18.1 %fusion.22 = f32[640,1152]{1,0:T(8,128)} fusion(bf16[6144,1152]{1,0:T(8,128)(2,1)} %all-gather.5.cloned.1.call-done, bf16[640,6144]{1,0:T(8,128)(2,1)} %all-gather.3.cloned.1.call-done, f32[6144]{0:T(1024)S(1)} %copy-done.17, f32[6144]{0:T(1024)S(1)} %copy-done.18, f32[640]{0:T(1024)S(1)} %add_rsqrt_fusion, f32[640]{0:T(1024)S(1)} %broadcast_multiply_fusion.1, ...), kind=kOutput, calls=%fused_computation.34 | convolution fusion | flops 9084026880 | bytes 25028096 | tf_op jit(solution)/shard_map/dot_general | solution.py:127
  182.0 3.1 copy.119
  185.3 1.3 copy_bitcast_fusion
  187.3 6.4 %gather_fusion = bf16[1920,384]{1,0:T(8,128)(2,1)S(1)} fusion(bf16[640,384]{1,0:T(8,128)(2,1)S(1)} %copy.121, s32[2048]{0:T(1024)S(1)} %pad_clamp_fusion), kind=kCustom, calls=%fused_computation | custom fusion | bytes 2956800 | tf_op jit(solution)/shard_map/gather | solution.py:148
  193.8 1.5 broadcast_select_fusion
  195.3 3.7 all-to-all-start
  199.0 19.7 %all-to-all-done = bf16[16,120,384]{2,1,0:T(8,128)(2,1)S(1)} async-done(((bf16[16,120,384]{2,1,0:T(8,128)(2,1)}), bf16[16,120,384]{2,1,0:T(8,128)(2,1)S(1)}, u32[]{:S(2)}, u32[]{:S(2)}) %all-to-all-start) | async-done | bytes 1474592 | tf_op jit(solution)/shard_map/all_to_all | solution.py:149
  218.7 1.3 copy.122
  219.9 158.2 %while.14 = (s32[]{:T(128)}, f32[2,960,384]{2,0,1:T(2,128)}, f32[2,960,4]{1,2,0:T(4,128)S(1)}, f32[2,960,4]{1,2,0:T(4,128)S(1)}, bf16[2,2048,384]{2,1,0:T(8,128)...) while((s32[]{:T(128)}, f32[2,960,384]{2,0,1:T(2,128)}, ...), condition=%wide.region_10.11_spmd, body=%wide.region_7.10_spmd.sunk | while | flops 3083174400 | bytes 127593616 | solution.py:150
  219.9 1.2 constant_dynamic-slice_fusion.7
  221.1 1.2 copy.166
  222.4 1.6 constant_dynamic-slice_fusion.8
  223.9 0.8 copy.167
  224.7 1.6 constant_dynamic-slice_fusion.6
  226.3 1.6 copy.165
  227.9 13.6 %multiply_reduce_fusion.2 = (f32[4,960]{1,0:T(4,128)S(1)}, f32[4,960,2048]{2,1,0:T(8,128)}) fusion(bf16[960,4,96]{0,2,1:T(8,128)(2,1)} %bitcast.96, bf16[2048,4,96]{0,2,1:T(8,128)(2,1)S(1)} %bitcast.95), kind=kOutput, calls=%fused_computation.5.clone.1 | convolution fusion | flops 1525674240 | bytes 33782784 | tf_op jit(solution)/shard_map/while/body/eval_jaxpr/rhd,phd->hrp/dot_general | solution.py:82
  241.5 13.8 %fusion.74 = f32[4,960]{1,0:T(4,128)S(1)} fusion(f32[4,960,2048]{2,1,0:T(8,128)} %get-tuple-element.176, f32[4,960]{1,0:T(4,128)S(1)} %get-tuple-element.177), kind=kLoop, calls=%fused_computation.6.clone.1 | loop fusion | flops 23589120 | bytes 31488000 | tf_op jit(solution)/shard_map/while/body/eval_jaxpr/reduce_sum | solution.py:87
  255.4 12.8 %bitcast_divide_fusion.2 = f32[960,4,96]{0,2,1:T(8,128)S(1)} fusion(bf16[2048,4,96]{0,2,1:T(8,128)(2,1)S(1)} %bitcast.97, f32[4,960,2048]{2,1,0:T(8,128)} %get-tuple-element.176, f32[4,960]{1,0:T(4,128)S(1)} %get-tuple-element.177, f32[960,4]{0,1:T(4,128)S(1)} %bitcast.113), kind=kOutput, calls=%fused_computation.9.clone.1 | convolution fusion | flops 1533911040 | bytes 34535424 | tf_op jit(solution)/shard_map/while/body/eval_jaxpr/hrp,phd->rhd/dot_general | solution.py:89
  268.2 2.3 copy.168
  270.5 28.5 %dynamic_update_slice.16 = f32[2,960,384]{2,0,1:T(2,128)} dynamic-update-slice(f32[2,960,384]{2,0,1:T(2,128)} %get-tuple-element.190, f32[1,960,384]{2,0,1:T(1,128)S(1)} %copy.168, s32[]{:T(128)S(6)} %copy.176, s32[]{:T(128)} %constant.26.clone.1..sunk, s32[]{:T(128)} %constant.26.clone.1..sunk) | dynamic-update-slice | bytes 2949124 | tf_op jit(solution)/shard_map/while/body/jit(dynamic_update_index_in_dim)/dynamic_update_slice | solution.py:150
  299.0 1.2 constant_dynamic-slice_fusion.7
  300.2 1.2 copy.166
  301.5 1.6 constant_dynamic-slice_fusion.8
  303.0 0.8 copy.167
  303.8 1.6 constant_dynamic-slice_fusion.6
  305.4 1.6 copy.165
  307.0 13.6 %multiply_reduce_fusion.2 = (f32[4,960]{1,0:T(4,128)S(1)}, f32[4,960,2048]{2,1,0:T(8,128)}) fusion(bf16[960,4,96]{0,2,1:T(8,128)(2,1)} %bitcast.96, bf16[2048,4,96]{0,2,1:T(8,128)(2,1)S(1)} %bitcast.95), kind=kOutput, calls=%fused_computation.5.clone.1 | convolution fusion | flops 1525674240 | bytes 33782784 | tf_op jit(solution)/shard_map/while/body/eval_jaxpr/rhd,phd->hrp/dot_general | solution.py:82
  320.6 13.8 %fusion.74 = f32[4,960]{1,0:T(4,128)S(1)} fusion(f32[4,960,2048]{2,1,0:T(8,128)} %get-tuple-element.176, f32[4,960]{1,0:T(4,128)S(1)} %get-tuple-element.177), kind=kLoop, calls=%fused_computation.6.clone.1 | loop fusion | flops 23589120 | bytes 31488000 | tf_op jit(solution)/shard_map/while/body/eval_jaxpr/reduce_sum | solution.py:87
  334.5 12.8 %bitcast_divide_fusion.2 = f32[960,4,96]{0,2,1:T(8,128)S(1)} fusion(bf16[2048,4,96]{0,2,1:T(8,128)(2,1)S(1)} %bitcast.97, f32[4,960,2048]{2,1,0:T(8,128)} %get-tuple-element.176, f32[4,960]{1,0:T(4,128)S(1)} %get-tuple-element.177, f32[960,4]{0,1:T(4,128)S(1)} %bitcast.113), kind=kOutput, calls=%fused_computation.9.clone.1 | convolution fusion | flops 1533911040 | bytes 34535424 | tf_op jit(solution)/shard_map/while/body/eval_jaxpr/hrp,phd->rhd/dot_general | solution.py:89
  347.3 2.3 copy.168
  349.6 28.5 %dynamic_update_slice.16 = f32[2,960,384]{2,0,1:T(2,128)} dynamic-update-slice(f32[2,960,384]{2,0,1:T(2,128)} %get-tuple-element.190, f32[1,960,384]{2,0,1:T(1,128)S(1)} %copy.168, s32[]{:T(128)S(6)} %copy.176, s32[]{:T(128)} %constant.26.clone.1..sunk, s32[]{:T(128)} %constant.26.clone.1..sunk) | dynamic-update-slice | bytes 2949124 | tf_op jit(solution)/shard_map/while/body/jit(dynamic_update_index_in_dim)/dynamic_update_slice | solution.py:150
  378.2 0.9 copy.126
  379.1 2.0 reshape.329
  381.2 4.1 all-to-all-start.1
  385.3 0.9 copy.128
  386.2 1.4 reshape.331
  387.6 2.4 all-to-all-done.1
  390.0 7.8 %all_to_all.63 = f32[8,1,960]{2,1,0:T(1,128)S(1)} all-to-all(f32[8,1,960]{2,1,0:T(1,128)S(1)} %reshape.331), channel_id=1, replica_groups=mesh['tok'=8,'head'=16] {'tok'}, dimensions={0} | all-to-all | bytes 61440 | tf_op jit(solution)/shard_map/all_to_all | solution.py:153
  397.8 5.1 all-to-all-start.3
  403.4 1.4 fusion.19
  404.7 2.7 copy-done.3
  407.5 1.4 fusion.21
  410.1 1.4 reshape.330
  411.7 1.7 gather_fusion.1
  413.5 0.7 reduce.2
  414.2 1.4 reshape.332
  415.7 1.7 gather_fusion.2
  417.6 20.9 %all-to-all-done.3 = f32[2,960,384]{2,0,1:T(2,128)} async-done(((f32[2,960,384]{2,0,1:T(2,128)}), f32[2,960,384]{2,0,1:T(2,128)}, u32[]{:S(2)}, u32[]{:S(2)}) %all-to-all-start.3) | async-done | bytes 2949152 | tf_op jit(solution)/shard_map/all_to_all | solution.py:152
  438.5 2.0 copy.135
  440.7 3.6 reshape.327
  444.3 3.9 gather_fusion.3
  448.2 1.0 copy.138
  449.2 5.3 divide_convert_fusion
  454.5 7.7 %fusion.56 = f32[640,6144]{1,0:T(8,128)} fusion(bf16[640,384]{0,1:T(8,128)(2,1)S(1)} %bitcast.114, bf16[384,6144]{1,0:T(8,128)(2,1)S(1)} %bitcast.107), kind=kOutput, calls=%fused_computation.98 | convolution fusion | flops 3019898880 | bytes 20938752 | tf_op jit(solution)/shard_map/dot_general | solution.py:168
  462.9 104.4 %reduce-scatter.2.cloned.1.call-done = f32[640,384]{1,0:T(8,128)} async-done(((f32[640,6144]{1,0:T(8,128)}), f32[640,384]{1,0:T(8,128)}) %reduce-scatter.2.cloned.1.call-update) | async-done | bytes 983056 | tf_op jit(solution)/shard_map/reduce_scatter | solution.py:169
  567.3 2.1 add_convert_fusion
  (85 shorter events, 8.5 us)
Async XLA Ops:
  6.5 81.1 %all-gather.3.cloned.1.call-start = ((), (), s32[]{:S(2)}) async-start(), calls=%async_computation.5 | async-start | bytes 8355840 | tf_op jit(solution)/shard_map/all_gather | solution.py:125
  7.3 156.7 %all-gather.5.cloned.1.call-start = ((), (), s32[]{:S(2)}) async-start(), calls=%async_computation.6 | async-start | bytes 15925248 | tf_op jit(solution)/shard_map/all_gather | solution.py:129
  13.2 0.7 copy-start.13
  14.1 172.4 %copy-start.8 = (f32[640,12]{0,1:T(8,128)}, f32[640,12]{0,1:T(8,128)S(1)}, u32[]{:S(2)}) copy-start(f32[640,12]{0,1:T(8,128)S(1)} %get-tuple-element.121) | copy-start | bytes 92164
  14.1 172.4 %copy-start.10 = (f32[640,12]{0,1:T(8,128)}, f32[640,12]{0,1:T(8,128)S(1)}, u32[]{:S(2)}) copy-start(f32[640,12]{0,1:T(8,128)S(1)} %get-tuple-element.122) | copy-start | bytes 92164
  87.7 5.5 copy-start.1
  87.7 76.2 %copy-start.17 = (f32[6144]{0:T(1024)S(1)}, f32[6144]{0:T(1024)}, u32[]{:S(2)}) copy-start(f32[6144]{0:T(1024)} %param.16) | copy-start | bytes 73732
  87.7 76.2 %copy-start.18 = (f32[6144]{0:T(1024)S(1)}, f32[6144]{0:T(1024)}, u32[]{:S(2)}) copy-start(f32[6144]{0:T(1024)} %param.15) | copy-start | bytes 73732
  185.1 1.9 copy-start.2
  187.0 6.7 %copy-start.6 = (bf16[640,4,96]{0,2,1:T(8,128)(2,1)}, bf16[640,4,96]{0,2,1:T(8,128)(2,1)S(1)}, u32[]{:S(2)}) copy-start(bf16[640,4,96]{0,2,1:T(8,128)(2,1)S(1)} %maximum_convert_fusion) | copy-start | bytes 1474564
  195.3 23.4 %all-to-all-start = ((bf16[16,120,384]{2,1,0:T(8,128)(2,1)}), bf16[16,120,384]{2,1,0:T(8,128)(2,1)S(1)}, u32[]{:S(2)}, u32[]{:S(2)}) async-start(bf16[16,120,384]{2,1,0:T(8,128)(2,1)} %broadcast_select_fusion), calls=%async_computation | async-start | bytes 2949120 | tf_op jit(solution)/shard_map/all_to_all | solution.py:149
  241.5 13.8 %copy-start = (bf16[1,2048,384]{1,2,0:T(8,128)(2,1)S(1)}, bf16[1,2048,384]{1,2,0:T(8,128)(2,1)}, u32[]{:S(2)}) copy-start(bf16[1,2048,384]{1,2,0:T(8,128)(2,1)} %copy.165) | copy-start | bytes 4718596 | tf_op jit(solution)/shard_map/while
  320.6 13.8 %copy-start = (bf16[1,2048,384]{1,2,0:T(8,128)(2,1)S(1)}, bf16[1,2048,384]{1,2,0:T(8,128)(2,1)}, u32[]{:S(2)}) copy-start(bf16[1,2048,384]{1,2,0:T(8,128)(2,1)} %copy.165) | copy-start | bytes 4718596 | tf_op jit(solution)/shard_map/while
  378.1 24.7 %copy-start.14 = (s32[640]{0:T(1024)S(1)}, s32[640]{0:T(1024)}, u32[]{:S(2)}) copy-start(s32[640]{0:T(1024)} %copy-done.13) | copy-start | bytes 7684
  378.1 24.7 %copy-start.15 = (s32[640]{0:T(1024)S(1)}, s32[640]{0:T(1024)}, u32[]{:S(2)}) copy-start(s32[640]{0:T(1024)} %get-tuple-element.128) | copy-start | bytes 7684
  378.1 24.8 %copy-start.12 = (s32[640]{0:T(1024)S(1)}, s32[640]{0:T(1024)}, u32[]{:S(2)}) copy-start(s32[640]{0:T(1024)} %get-tuple-element.89) | copy-start | bytes 7684
  378.1 25.1 %copy-start.4 = (f32[640,4,96]{0,2,1:T(8,128)S(1)}, f32[640,4,96]{0,2,1:T(8,128)}, u32[]{:S(2)}) copy-start(f32[640,4,96]{0,2,1:T(8,128)} %get-tuple-element.125) | copy-start | bytes 2949124
  378.1 25.1 %copy-start.9 = (f32[640,12]{0,1:T(8,128)S(1)}, f32[640,12]{0,1:T(8,128)}, u32[]{:S(2)}) copy-start(f32[640,12]{0,1:T(8,128)} %copy-done.8) | copy-start | bytes 92164
  378.2 25.1 %copy-start.11 = (f32[640,12]{0,1:T(8,128)S(1)}, f32[640,12]{0,1:T(8,128)}, u32[]{:S(2)}) copy-start(f32[640,12]{0,1:T(8,128)} %copy-done.10) | copy-start | bytes 92164
  378.2 25.2 %copy-start.7 = (bf16[640,4,96]{0,2,1:T(8,128)(2,1)S(1)}, bf16[640,4,96]{0,2,1:T(8,128)(2,1)}, u32[]{:S(2)}) copy-start(bf16[640,4,96]{0,2,1:T(8,128)(2,1)} %copy-done.6) | copy-start | bytes 1474564
  381.2 8.8 %all-to-all-start.1 = ((f32[8,1,960]{2,1,0:T(1,128)}), f32[8,1,960]{2,1,0:T(1,128)S(1)}, u32[]{:S(2)}, u32[]{:S(2)}) async-start(f32[8,1,960]{2,1,0:T(1,128)} %reshape.329), calls=%async_computation.1 | async-start | bytes 65536 | tf_op jit(solution)/shard_map/all_to_all | solution.py:154
  397.8 40.6 %all-to-all-start.3 = ((f32[2,960,384]{2,0,1:T(2,128)}), f32[2,960,384]{2,0,1:T(2,128)}, u32[]{:S(2)}, u32[]{:S(2)}) async-start(f32[2,960,384]{2,0,1:T(2,128)} %get-tuple-element.46), calls=%async_computation.3 | async-start | bytes 5898240 | tf_op jit(solution)/shard_map/all_to_all | solution.py:152
  402.9 164.4 %reduce-scatter.2.cloned.1.call-start = ((), (), s32[]{:S(2)}) async-start(), calls=%async_computation.7 | async-start | bytes 16711680 | tf_op jit(solution)/shard_map/reduce_scatter | solution.py:169
  404.7 2.7 copy-start.3
  448.2 6.3 %slice-start = ((s8[4718592]{0:T(1024)(128)(4,1)}), s8[524288]{0:T(1024)(128)(4,1)S(1)}, s32[]{:S(2)}) async-start(s8[4718592]{0:T(1024)(128)(4,1)} %bitcast.106), calls=%async_computation.8 | async-start | bytes 1048576
  449.2 5.3 slice-start.1
  462.2 0.7 copy-start.16
  462.2 105.1 %copy-start.5 = (bf16[640,384]{1,0:T(8,128)(2,1)S(1)}, bf16[640,384]{1,0:T(8,128)(2,1)}, u32[]{:S(2)}) copy-start(bf16[640,384]{1,0:T(8,128)(2,1)} %param.14) | copy-start | bytes 1474564
Sparse Core Ops, SparseCore 0:
  9.5 78.1 all-gather.2
  89.4 74.5 all-gather.4
  462.4 104.8 reduce-scatter.1
where the time goes:
time: 581 us; the launch traced here: 576 us
  waiting for transfers between devices  291 us (50%)
  local copies, waits for them, and re-layouts  118 us (20%)
  matrix products  85.3 us (15%)
  other arithmetic  47.4 us (8%)
  between operations  13.5 us (2%)
  starting transfers between devices  12.9 us (2%)
  blocking collectives  7.8 us (1%)
    reduce_scatter x1, waiting for transfers between devices, on_device(): lax.psum_scatter(partial_out, 'head', scatter_dimension=1, tiled=True)  104 us
    all_gather x1, waiting for transfers between devices, on_device(): full_rows = lax.all_gather(hidden_states, 'head', axis=1, tiled=True)  73.5 us
    all_gather x1, waiting for transfers between devices, on_device(): lax.all_gather(qkv_weight, 'tok', axis=0, tiled=True)  68.6 us
    dynamic_update_slice x6, local copies, waits for them, and re-layouts, on_device(): lax.map(prefix_slot, (incoming, prefix_keys, prefix_values))  61.7 us
    reduce_sum x2, other arithmetic, prefix_slot(): row_mass = jnp.sum(weights, axis=-1)  27.7 us
    dot_general x2, matrix products, prefix_slot(): jnp.einsum('rhd,phd->hrp', query_heads, key_heads, preferred_element_type...  27.2 us
    dot_general x2, matrix products, prefix_slot(): jnp.einsum('hrp,phd->rhd', weights.astype(jnp.bfloat16), value_heads, pre...  25.6 us
    all_to_all x1, waiting for transfers between devices, on_device(): lax.all_to_all(pre_all, 'tok', split_axis=1, concat_axis=0, tiled=True)  20.9 us
  transfers between devices with their start and end apart: 6, of which 6 were waited for; matrix products, arithmetic and copies ran while one was open for 5% of the time, Pallas kernels for 0%

commit v1 on v0

--- a/solution.py
+++ b/solution.py
@@ -149,7 +149,12 @@
     incoming = lax.all_to_all(outgoing, "tok", split_axis=0, concat_axis=1, tiled=True)
     pre_all, peak_all, mass_all = lax.map(prefix_slot, (incoming, prefix_keys, prefix_values))
     returned = (
-        lax.all_to_all(pre_all, "tok", split_axis=1, concat_axis=0, tiled=True),
+        jnp.concatenate(
+            lax.all_to_all(
+                jnp.stack(jnp.split(pre_all, lax.axis_size("tok"), axis=1)), "tok", 0, 0
+            ),
+            axis=0,
+        ),
         lax.all_to_all(peak_all, "tok", split_axis=1, concat_axis=0, tiled=True),
         lax.all_to_all(mass_all, "tok", split_axis=1, concat_axis=0, tiled=True),
     )

time: 581 us -> 528 us (0.909)
  local copies, waits for them, and re-layouts: 118 us -> 71.5 us
  blocking collectives: 7.8 us -> 0 us
    dynamic_update_slice x6, local copies, waits for them, and re-layouts: 61.7 us -> 3.4 us  [on_device(): lax.map(prefix_slot, (incoming, prefix_keys, prefix_values))]
    unnamed x44 -> x53, local copies, waits for them, and re-layouts: 11.1 us -> 21.4 us
    all_to_all x1 -> x0, blocking collectives: 7.8 us -> none  [on_device(): lax.all_to_all(peak_all, 'tok', split_axis=1, concat_axis=0, tiled=True)]
    another operation x0 -> x2, local copies, waits for them, and re-layouts: none -> 7.25 us  [the longest x1 5.47 us: on_device(): returned[0].reshape(group_count * capacity, local_heads, HS)[flat_index]]
    all_to_all x1 -> x2, waiting for transfers between devices: 20.9 us -> 23.8 us  [the longest x1 20.9 us: on_device(): lax.all_to_all(jnp.stack(jnp.split(pre_all, lax.axis_size('tok'), axis=1)...]
  transfers between devices with their start and end apart: 6 -> 7, of which waited for: 6 -> 6; matrix products, arithmetic and copies ran while one was open for 5% -> 7% of each run, Pallas kernels for 0% -> 0%
where the time goes in v1:
time: 528 us; the launch traced here: 527 us
  waiting for transfers between devices  291 us (55%)
  matrix products  85.1 us (16%)
  local copies, waits for them, and re-layouts  71.5 us (14%)
  other arithmetic  47.4 us (9%)
  starting transfers between devices  17.8 us (3%)
  between operations  13.5 us (3%)
    reduce_scatter x1, waiting for transfers between devices, on_device(): lax.psum_scatter(partial_out, 'head', scatter_dimension=1, tiled=True)  104 us
    all_gather x1, waiting for transfers between devices, on_device(): full_rows = lax.all_gather(hidden_states, 'head', axis=1, tiled=True)  73.5 us
    all_gather x1, waiting for transfers between devices, on_device(): lax.all_gather(qkv_weight, 'tok', axis=0, tiled=True)  68.6 us
    reduce_sum x2, other arithmetic, prefix_slot(): row_mass = jnp.sum(weights, axis=-1)  27.7 us
    dot_general x2, matrix products, prefix_slot(): jnp.einsum('rhd,phd->hrp', query_heads, key_heads, preferred_element_type...  27 us
    dot_general x2, matrix products, prefix_slot(): jnp.einsum('hrp,phd->rhd', weights.astype(jnp.bfloat16), value_heads, pre...  25.5 us
    unnamed x53, local copies, waits for them, and re-layouts  21.4 us
    all_to_all x1, waiting for transfers between devices, on_device(): lax.all_to_all(jnp.stack(jnp.split(pre_all, lax.axis_size('tok'), axis=1)...  20.9 us
  transfers between devices with their start and end apart: 7, of which 6 were waited for; matrix products, arithmetic and copies ran while one was open for 7% of the time, Pallas kernels for 0%

profile of v1, /device:TPU:1, one launch (start us, length us, event | category | flops | bytes accessed | tf_op | source)
XLA Modules:
  0.0 526.8 jit_solution(8482174251086948851)
XLA Ops:
  11.9 1.3 select_reduce_fusion
  14.2 73.5 %all-gather.3.cloned.1.call-done = bf16[640,6144]{1,0:T(8,128)(2,1)} async-done(((bf16[640,384]{1,0:T(8,128)(2,1)}), bf16[640,6144]{1,0:T(8,128)(2,1)}) %all-gather.3.cloned.1.call-update) | async-done | bytes 7864336 | tf_op jit(solution)/shard_map/all_gather | solution.py:125
  87.7 4.5 convert_reduce_fusion
  92.2 1.0 copy-done.1
  93.1 2.2 fusion.9
  95.3 68.6 %all-gather.5.cloned.1.call-done = bf16[6144,1152]{1,0:T(8,128)(2,1)} async-done(((bf16[768,1152]{1,0:T(8,128)(2,1)}), bf16[6144,1152]{1,0:T(8,128)(2,1)}) %all-gather.5.cloned.1.call-update) | async-done | bytes 14155792 | tf_op jit(solution)/shard_map/all_gather | solution.py:129
  163.9 18.1 %fusion.22 = f32[640,1152]{1,0:T(8,128)} fusion(bf16[6144,1152]{1,0:T(8,128)(2,1)} %all-gather.5.cloned.1.call-done, bf16[640,6144]{1,0:T(8,128)(2,1)} %all-gather.3.cloned.1.call-done, f32[6144]{0:T(1024)S(1)} %copy-done.18, f32[6144]{0:T(1024)S(1)} %copy-done.19, f32[640]{0:T(1024)S(1)} %add_rsqrt_fusion, f32[640]{0:T(1024)S(1)} %broadcast_multiply_fusion.1, ...), kind=kOutput, calls=%fused_computation.35 | convolution fusion | flops 9084026880 | bytes 25028096 | tf_op jit(solution)/shard_map/dot_general | solution.py:127
  182.0 3.1 copy.129
  185.2 1.3 copy_bitcast_fusion
  188.3 6.4 %gather_fusion = bf16[1920,384]{1,0:T(8,128)(2,1)S(1)} fusion(bf16[640,384]{1,0:T(8,128)(2,1)S(1)} %copy.131, s32[2048]{0:T(1024)S(1)} %pad_clamp_fusion), kind=kCustom, calls=%fused_computation | custom fusion | bytes 2956800 | tf_op jit(solution)/shard_map/gather | solution.py:148
  194.7 1.5 broadcast_select_fusion
  196.2 3.7 all-to-all-start
  199.9 19.7 %all-to-all-done = bf16[16,120,384]{2,1,0:T(8,128)(2,1)S(1)} async-done(((bf16[16,120,384]{2,1,0:T(8,128)(2,1)}), bf16[16,120,384]{2,1,0:T(8,128)(2,1)S(1)}, u32[]{:S(2)}, u32[]{:S(2)}) %all-to-all-start) | async-done | bytes 1474592 | tf_op jit(solution)/shard_map/all_to_all | solution.py:149
  219.6 1.3 copy.132
  220.8 99.7 %while.14 = (s32[]{:T(128)}, f32[2,960,384]{2,1,0:T(8,128)}, f32[2,960,4]{1,2,0:T(4,128)S(1)}, f32[2,960,4]{1,2,0:T(4,128)S(1)}, bf16[2,2048,384]{2,1,0:T(8,128)...) while((s32[]{:T(128)}, f32[2,960,384]{2,1,0:T(8,128)}, ...), condition=%wide.region_10.11_spmd, body=%wide.region_7.10_spmd.sunk | while | flops 3083174400 | bytes 127593608 | solution.py:150
  220.8 1.2 constant_dynamic-slice_fusion.7
  222.0 1.2 copy.181
  223.3 1.6 constant_dynamic-slice_fusion.8
  225.6 1.6 constant_dynamic-slice_fusion.6
  227.2 1.7 copy.180
  228.8 13.5 %multiply_reduce_fusion.2 = (f32[4,960]{1,0:T(4,128)S(1)}, f32[4,960,2048]{2,1,0:T(8,128)}) fusion(bf16[960,4,96]{0,2,1:T(8,128)(2,1)} %bitcast.109, bf16[2048,4,96]{0,2,1:T(8,128)(2,1)S(1)} %bitcast.108), kind=kOutput, calls=%fused_computation.5.clone.1 | convolution fusion | flops 1525674240 | bytes 33782784 | tf_op jit(solution)/shard_map/while/body/eval_jaxpr/rhd,phd->hrp/dot_general | solution.py:82
  242.4 13.8 %fusion.74 = f32[4,960]{1,0:T(4,128)S(1)} fusion(f32[4,960,2048]{2,1,0:T(8,128)} %get-tuple-element.176, f32[4,960]{1,0:T(4,128)S(1)} %get-tuple-element.177), kind=kLoop, calls=%fused_computation.6.clone.1 | loop fusion | flops 23589120 | bytes 31488000 | tf_op jit(solution)/shard_map/while/body/eval_jaxpr/reduce_sum | solution.py:87
  256.2 12.8 %bitcast_divide_fusion.2 = f32[960,4,96]{0,2,1:T(8,128)S(1)} fusion(bf16[2048,4,96]{0,2,1:T(8,128)(2,1)S(1)} %bitcast.110, f32[4,960,2048]{2,1,0:T(8,128)} %get-tuple-element.176, f32[4,960]{1,0:T(4,128)S(1)} %get-tuple-element.177, f32[960,4]{0,1:T(4,128)S(1)} %bitcast.125), kind=kOutput, calls=%fused_computation.9.clone.1 | convolution fusion | flops 1533911040 | bytes 34535424 | tf_op jit(solution)/shard_map/while/body/eval_jaxpr/hrp,phd->rhd/dot_general | solution.py:89
  269.5 1.2 constant_dynamic-update-slice_fusion.2
  270.7 1.2 constant_dynamic-slice_fusion.7
  271.9 1.2 copy.181
  273.1 1.6 constant_dynamic-slice_fusion.8
  275.4 1.6 constant_dynamic-slice_fusion.6
  277.0 1.7 copy.180
  278.7 13.5 %multiply_reduce_fusion.2 = (f32[4,960]{1,0:T(4,128)S(1)}, f32[4,960,2048]{2,1,0:T(8,128)}) fusion(bf16[960,4,96]{0,2,1:T(8,128)(2,1)} %bitcast.109, bf16[2048,4,96]{0,2,1:T(8,128)(2,1)S(1)} %bitcast.108), kind=kOutput, calls=%fused_computation.5.clone.1 | convolution fusion | flops 1525674240 | bytes 33782784 | tf_op jit(solution)/shard_map/while/body/eval_jaxpr/rhd,phd->hrp/dot_general | solution.py:82
  292.2 13.8 %fusion.74 = f32[4,960]{1,0:T(4,128)S(1)} fusion(f32[4,960,2048]{2,1,0:T(8,128)} %get-tuple-element.176, f32[4,960]{1,0:T(4,128)S(1)} %get-tuple-element.177), kind=kLoop, calls=%fused_computation.6.clone.1 | loop fusion | flops 23589120 | bytes 31488000 | tf_op jit(solution)/shard_map/while/body/eval_jaxpr/reduce_sum | solution.py:87
  306.1 12.8 %bitcast_divide_fusion.2 = f32[960,4,96]{0,2,1:T(8,128)S(1)} fusion(bf16[2048,4,96]{0,2,1:T(8,128)(2,1)S(1)} %bitcast.110, f32[4,960,2048]{2,1,0:T(8,128)} %get-tuple-element.176, f32[4,960]{1,0:T(4,128)S(1)} %get-tuple-element.177, f32[960,4]{0,1:T(4,128)S(1)} %bitcast.125), kind=kOutput, calls=%fused_computation.9.clone.1 | convolution fusion | flops 1533911040 | bytes 34535424 | tf_op jit(solution)/shard_map/while/body/eval_jaxpr/hrp,phd->rhd/dot_general | solution.py:89
  319.3 1.2 constant_dynamic-update-slice_fusion.2
  320.6 0.9 copy.136
  321.5 2.0 reshape.324
  323.5 4.1 all-to-all-start.1
  327.6 1.0 bitcast_dynamic-update-slice_fusion.9
  328.6 1.0 bitcast_dynamic-update-slice_fusion.8
  329.7 1.0 bitcast_dynamic-update-slice_fusion.7
  330.7 1.0 bitcast_dynamic-update-slice_fusion.6
  331.7 1.0 bitcast_dynamic-update-slice_fusion.5
  332.7 1.0 bitcast_dynamic-update-slice_fusion.4
  333.8 1.0 bitcast_dynamic-update-slice_fusion.3
  334.8 1.6 copy-done.4
  337.3 2.0 reshape.326
  339.4 4.8 all-to-all-start.2
  344.2 1.8 bitcast_dynamic-update-slice_fusion.2
  346.0 2.9 all-to-all-done.2
  348.9 5.1 all-to-all-start.3
  354.5 1.4 fusion.19
  355.8 2.7 copy-done.3
  358.6 1.4 fusion.21
  361.3 1.4 reshape.325
  362.8 1.7 gather_fusion.1
  365.3 1.4 reshape.327
  366.8 1.7 gather_fusion.2
  368.7 20.9 %all-to-all-done.3 = f32[8,2,120,384]{3,2,1,0:T(8,128)} async-done(((f32[8,2,120,384]{3,2,1,0:T(8,128)}), f32[8,2,120,384]{3,2,1,0:T(8,128)}, u32[]{:S(2)}, u32[]{:S(2)}) %all-to-all-start.3) | async-done | bytes 2949152 | tf_op jit(solution)/shard_map/all_to_all | solution.py:153
  389.6 5.5 %reshape.322 = f32[1920,4,96]{2,1,0:T(4,128)} reshape(f32[8,2,120,384]{3,2,1,0:T(8,128)} %all-to-all-done.3) | data formatting | bytes 5898240 | tf_op jit(solution)/shard_map/reshape;reshape | solution.py:163
  395.0 3.9 gather_fusion.3
  398.9 1.0 copy.154
  399.9 5.3 %divide_convert_fusion = bf16[640,4,96]{0,2,1:T(8,128)(2,1)S(1)} fusion(f32[640,4,96]{0,2,1:T(8,128)S(1)} %copy.154, f32[4,640,640]{1,2,0:T(8,128)} %copy-done.3, f32[4,640]{1,0:T(4,128)S(1)} %get-tuple-element.123, pred[640,640]{0,1:T(8,128)(4,1)S(1)} %fusion.28, f32[640,4]{0,1:T(4,128)S(1)} %get-tuple-element.108, f32[640,4]{0,1:T(4,128)S(1)} %bitcast.127, ...), kind=kOutput, calls=%fused_computation.47 | convolution fusion | flops 322600960 | bytes 8980480 | tf_op jit(solution)/shard_map/hij,jhd->ihd/dot_general | solution.py:62
  405.2 7.8 %fusion.56 = f32[640,6144]{1,0:T(8,128)} fusion(bf16[640,384]{0,1:T(8,128)(2,1)S(1)} %bitcast.126, bf16[384,6144]{1,0:T(8,128)(2,1)S(1)} %bitcast.119), kind=kOutput, calls=%fused_computation.107 | convolution fusion | flops 3019898880 | bytes 20938752 | tf_op jit(solution)/shard_map/dot_general | solution.py:173
  413.7 104.5 %reduce-scatter.2.cloned.1.call-done = f32[640,384]{1,0:T(8,128)} async-done(((f32[640,6144]{1,0:T(8,128)}), f32[640,384]{1,0:T(8,128)}) %reduce-scatter.2.cloned.1.call-update) | async-done | bytes 983056 | tf_op jit(solution)/shard_map/reduce_scatter | solution.py:174
  518.1 2.1 add_convert_fusion
  (94 shorter events, 15.0 us)
Async XLA Ops:
  6.5 81.1 %all-gather.3.cloned.1.call-start = ((), (), s32[]{:S(2)}) async-start(), calls=%async_computation.5 | async-start | bytes 8355840 | tf_op jit(solution)/shard_map/all_gather | solution.py:125
  7.3 156.7 %all-gather.5.cloned.1.call-start = ((), (), s32[]{:S(2)}) async-start(), calls=%async_computation.6 | async-start | bytes 15925248 | tf_op jit(solution)/shard_map/all_gather | solution.py:129
  13.2 0.7 copy-start.14
  14.1 172.9 %copy-start.9 = (f32[640,12]{0,1:T(8,128)}, f32[640,12]{0,1:T(8,128)S(1)}, u32[]{:S(2)}) copy-start(f32[640,12]{0,1:T(8,128)S(1)} %get-tuple-element.121) | copy-start | bytes 92164
  14.1 172.9 %copy-start.11 = (f32[640,12]{0,1:T(8,128)}, f32[640,12]{0,1:T(8,128)S(1)}, u32[]{:S(2)}) copy-start(f32[640,12]{0,1:T(8,128)S(1)} %get-tuple-element.122) | copy-start | bytes 92164
  87.7 5.5 %copy-start.1 = (bf16[640,6144]{1,0:T(8,128)(2,1)S(1)}, bf16[640,6144]{1,0:T(8,128)(2,1)}, u32[]{:S(2)}) copy-start(bf16[640,6144]{1,0:T(8,128)(2,1)} %all-gather.3.cloned.1.call-done) | copy-start | bytes 23592964
  93.1 70.8 %copy-start.18 = (f32[6144]{0:T(1024)S(1)}, f32[6144]{0:T(1024)}, u32[]{:S(2)}) copy-start(f32[6144]{0:T(1024)} %param.16) | copy-start | bytes 73732
  93.1 70.8 %copy-start.19 = (f32[6144]{0:T(1024)S(1)}, f32[6144]{0:T(1024)}, u32[]{:S(2)}) copy-start(f32[6144]{0:T(1024)} %param.15) | copy-start | bytes 73732
  185.1 1.9 copy-start.2
  187.2 0.8 copy-start.7
  196.2 23.4 %all-to-all-start = ((bf16[16,120,384]{2,1,0:T(8,128)(2,1)}), bf16[16,120,384]{2,1,0:T(8,128)(2,1)S(1)}, u32[]{:S(2)}, u32[]{:S(2)}) async-start(bf16[16,120,384]{2,1,0:T(8,128)(2,1)} %broadcast_select_fusion), calls=%async_computation | async-start | bytes 2949120 | tf_op jit(solution)/shard_map/all_to_all | solution.py:149
  242.4 13.8 %copy-start = (bf16[1,2048,384]{1,2,0:T(8,128)(2,1)S(1)}, bf16[1,2048,384]{1,2,0:T(8,128)(2,1)}, u32[]{:S(2)}) copy-start(bf16[1,2048,384]{1,2,0:T(8,128)(2,1)} %copy.180) | copy-start | bytes 4718596 | tf_op jit(solution)/shard_map/while
  292.2 13.8 %copy-start = (bf16[1,2048,384]{1,2,0:T(8,128)(2,1)S(1)}, bf16[1,2048,384]{1,2,0:T(8,128)(2,1)}, u32[]{:S(2)}) copy-start(bf16[1,2048,384]{1,2,0:T(8,128)(2,1)} %copy.180) | copy-start | bytes 4718596 | tf_op jit(solution)/shard_map/while
  323.5 15.8 %all-to-all-start.1 = ((f32[8,1,960]{2,1,0:T(1,128)}), f32[8,1,960]{2,1,0:T(1,128)S(1)}, u32[]{:S(2)}, u32[]{:S(2)}) async-start(f32[8,1,960]{2,1,0:T(1,128)} %reshape.324), calls=%async_computation.1 | async-start | bytes 65536 | tf_op jit(solution)/shard_map/all_to_all | solution.py:159
  334.8 1.6 copy-start.4
  339.4 9.5 %all-to-all-start.2 = ((f32[8,1,960]{2,1,0:T(1,128)}), f32[8,1,960]{2,1,0:T(1,128)S(1)}, u32[]{:S(2)}, u32[]{:S(2)}) async-start(f32[8,1,960]{2,1,0:T(1,128)} %reshape.326), calls=%async_computation.2 | async-start | bytes 65536 | tf_op jit(solution)/shard_map/all_to_all | solution.py:158
  346.0 8.0 %copy-start.15 = (s32[640]{0:T(1024)S(1)}, s32[640]{0:T(1024)}, u32[]{:S(2)}) copy-start(s32[640]{0:T(1024)} %copy-done.14) | copy-start | bytes 7684
  346.0 8.0 %copy-start.16 = (s32[640]{0:T(1024)S(1)}, s32[640]{0:T(1024)}, u32[]{:S(2)}) copy-start(s32[640]{0:T(1024)} %get-tuple-element.128) | copy-start | bytes 7684
  346.0 8.1 %copy-start.13 = (s32[640]{0:T(1024)S(1)}, s32[640]{0:T(1024)}, u32[]{:S(2)}) copy-start(s32[640]{0:T(1024)} %get-tuple-element.89) | copy-start | bytes 7684
  346.0 8.3 %copy-start.5 = (f32[640,4,96]{0,2,1:T(8,128)S(1)}, f32[640,4,96]{0,2,1:T(8,128)}, u32[]{:S(2)}) copy-start(f32[640,4,96]{0,2,1:T(8,128)} %get-tuple-element.125) | copy-start | bytes 2949124
  346.0 8.4 %copy-start.10 = (f32[640,12]{0,1:T(8,128)S(1)}, f32[640,12]{0,1:T(8,128)}, u32[]{:S(2)}) copy-start(f32[640,12]{0,1:T(8,128)} %copy-done.9) | copy-start | bytes 92164
  346.0 8.4 %copy-start.12 = (f32[640,12]{0,1:T(8,128)S(1)}, f32[640,12]{0,1:T(8,128)}, u32[]{:S(2)}) copy-start(f32[640,12]{0,1:T(8,128)} %copy-done.11) | copy-start | bytes 92164
  346.0 8.5 %copy-start.8 = (bf16[640,4,96]{0,2,1:T(8,128)(2,1)S(1)}, bf16[640,4,96]{0,2,1:T(8,128)(2,1)}, u32[]{:S(2)}) copy-start(bf16[640,4,96]{0,2,1:T(8,128)(2,1)} %copy-done.7) | copy-start | bytes 1474564
  348.9 40.6 %all-to-all-start.3 = ((f32[8,2,120,384]{3,2,1,0:T(8,128)}), f32[8,2,120,384]{3,2,1,0:T(8,128)}, u32[]{:S(2)}, u32[]{:S(2)}) async-start(f32[8,2,120,384]{3,2,1,0:T(8,128)} %bitcast_dynamic-update-slice_fusion.2), calls=%async_computation.3 | async-start | bytes 5898240 | tf_op jit(solution)/shard_map/all_to_all | solution.py:153
  354.0 164.2 %reduce-scatter.2.cloned.1.call-start = ((), (), s32[]{:S(2)}) async-start(), calls=%async_computation.7 | async-start | bytes 16711680 | tf_op jit(solution)/shard_map/reduce_scatter | solution.py:174
  355.8 2.8 copy-start.3
  398.9 6.3 %slice-start = ((s8[4718592]{0:T(1024)(128)(4,1)}), s8[524288]{0:T(1024)(128)(4,1)S(1)}, s32[]{:S(2)}) async-start(s8[4718592]{0:T(1024)(128)(4,1)} %bitcast.118), calls=%async_computation.8 | async-start | bytes 1048576
  399.9 5.3 %slice-start.1 = ((s8[4718592]{0:T(1024)(128)(4,1)}), s8[4194304]{0:T(1024)(128)(4,1)S(1)}, s32[]{:S(2)}) async-start(s8[4718592]{0:T(1024)(128)(4,1)} %bitcast.118), calls=%async_computation.9 | async-start | bytes 8388608
  413.0 0.7 copy-start.17
  413.0 105.2 %copy-start.6 = (bf16[640,384]{1,0:T(8,128)(2,1)S(1)}, bf16[640,384]{1,0:T(8,128)(2,1)}, u32[]{:S(2)}) copy-start(bf16[640,384]{1,0:T(8,128)(2,1)} %param.14) | copy-start | bytes 1474564
Sparse Core Ops, SparseCore 0:
  9.5 78.1 all-gather.2
  89.4 74.5 all-gather.4
  413.1 104.9 reduce-scatter.1
